TPU v7x, 32 devices: a whole 2x2x4 slice. The times are simulated.
32 devices in a mesh: mode: 8 (over z, x), row: 4 (over y, core).
Axes of the slice: x: 2, y: 2, z: 4, core: 2. Of those that a mesh axis runs over, the one named last changes fastest.
Arguments:
- forward: bfloat16 [64, 8, 2, 512], P('mode', 'row'), may hold values from -6 to 6
- backward: bfloat16 [64, 8, 2, 512], P('mode', 'row'), may hold values from -6 to 6
- propagator: bfloat16 [2, 512, 512], replicated, may hold values from -0.1875 to 0.1875
- row_taps: float32 [2, 3], replicated, may hold values from -3 to 3
- phase_masks: float32 [7, 8, 512], P(None, 'row'), may hold values from -3.140625 to 3.140625
- plane_index: int32 [4], replicated, may hold values from 0 to 6
- wave_ratio: float32 [4], replicated, may hold values from 0.7 to 1.4
- pair_list: int32 [80, 2], replicated, may hold values from 0 to 15, as said below
Outputs:
- coupling: float32 [2, 64, 64], P(None, 'mode')
- mask_grad: float32 [4, 8, 512], P(None, 'row')
Inputs may be any that keep to these rules, and one draw needn't show every extreme that they name: `pair_list`: each row names a target group and a forward group; no pair appears twice and every group is paired with itself; 80 pairs in all.
All inputs are finite; a program needn't handle non-finite values.
Results may differ from a plain program's by a relative error of at most 0.0078.
Values may be sent and summed in bfloat16 or wider, within the bound.
No kernel may reach another device: no remote copies, remote signals or barrier semaphores. Data moves between devices by JAX's collectives and lax.ppermute only.
A program may use at most 64 MiB of HBM per device.

v0:
```python
import math
import jax
import jax.numpy as jnp
from jax import lax
from jax.sharding import PartitionSpec as P

NG = 16


def padded_2(array, sides, width):
    for axis, dim in sides:
        peers, length = (lax.axis_size(axis), array.shape[dim])
        up = [(i, (i + 1) % peers) for i in range(peers - 1)]
        down = [(j, i) for i, j in up]
        last = lax.slice_in_dim(array, length - width, length, axis=dim)
        leading = lax.slice_in_dim(array, 0, width, axis=dim)
        before = lax.ppermute(last, axis, up)
        after = lax.ppermute(leading, axis, down)
        array = jnp.concatenate([before, array, after], axis=dim)
    return array


def chosen_phases(phase_masks, plane_index, wave_ratio):
    planes = jnp.arange(phase_masks.shape[0], dtype=jnp.int32)
    selector = (plane_index[:, None] == planes[None, :]).astype(jnp.float32)
    picked = jnp.einsum("wp,prc->wrc", selector, phase_masks, precision=lax.Precision.HIGHEST)
    return picked * wave_ratio[:, None, None]


def apply_mask(forward, phases):
    mode_total, row_total, _, width = forward.shape
    wave_total = phases.shape[0]
    shaped = forward.astype(jnp.float32).reshape(
        mode_total // wave_total, wave_total, row_total, 2, width
    )
    cosine = jnp.cos(phases)[None]
    sine = jnp.sin(phases)[None]
    real_part = shaped[:, :, :, 0] * cosine - shaped[:, :, :, 1] * sine
    imag_part = shaped[:, :, :, 0] * sine + shaped[:, :, :, 1] * cosine
    return jnp.stack([real_part, imag_part], axis=3).reshape(forward.shape).astype(jnp.bfloat16)


def forward_matrix(propagator):
    top_half = jnp.concatenate([propagator[0], propagator[1]], axis=1)
    low_half = jnp.concatenate([-propagator[1], propagator[0]], axis=1)
    return jnp.concatenate([top_half, low_half], axis=0)


def backward_matrix(propagator):
    top_half = jnp.concatenate([propagator[0].T, -propagator[1].T], axis=1)
    low_half = jnp.concatenate([propagator[1].T, propagator[0].T], axis=1)
    return jnp.concatenate([top_half, low_half], axis=0)


def propagate(fields, matrix):
    width = fields.shape[-1]
    result = jnp.dot(fields.reshape(-1, 2 * width), matrix, preferred_element_type=jnp.float32)
    return result.reshape(fields.shape)


def row_stencil(padded, row_taps, adjoint):
    values = padded.astype(jnp.float32)
    below_rows = values[:, :-2]
    center = values[:, 1:-1]
    above_rows = values[:, 2:]
    tap_real = row_taps[0]
    tap_imag = row_taps[1]
    if adjoint:
        sources = (above_rows, center, below_rows)
        tap_imag = -tap_imag
    else:
        sources = (below_rows, center, above_rows)
    real_sum = jnp.zeros(center[:, :, 0].shape, jnp.float32)
    imag_sum = jnp.zeros(center[:, :, 0].shape, jnp.float32)
    for position in range(3):
        source = sources[position]
        real_sum = (
            real_sum + tap_real[position] * source[:, :, 0] - tap_imag[position] * source[:, :, 1]
        )
        imag_sum = (
            imag_sum + tap_real[position] * source[:, :, 1] + tap_imag[position] * source[:, :, 0]
        )
    return jnp.stack([real_sum, imag_sum], axis=2)


def times_i(fields):
    return jnp.stack([-fields[:, :, 1], fields[:, :, 0]], axis=2)


def times_minus_i(fields):
    return jnp.stack([fields[:, :, 1], -fields[:, :, 0]], axis=2)


def body(forward, backward, propagator, row_taps, phase_masks, plane_index, wave_ratio, pair_list):
    local_modes, local_rows, _, width = forward.shape
    wave_total = wave_ratio.shape[0]
    mode_total = local_modes * lax.axis_size("mode")
    row_total = local_rows * lax.axis_size("row")
    group_size = mode_total // NG
    phases = chosen_phases(phase_masks, plane_index, wave_ratio)
    masked = apply_mask(forward, phases)
    spread = propagate(masked, forward_matrix(propagator)).astype(jnp.bfloat16)
    padded = padded_2(spread, (("row", 1),), 1)
    field = row_stencil(padded, row_taps, False).astype(jnp.bfloat16)
    field_flat = field.reshape(local_modes, -1)
    field_turned = times_minus_i(field).reshape(local_modes, -1)
    group_ids = jnp.arange(NG, dtype=jnp.int32)
    hits = (pair_list[:, 0][:, None, None] == group_ids[None, :, None]) & (
        pair_list[:, 1][:, None, None] == group_ids[None, None, :]
    )
    pair_matrix = jnp.sum(hits.astype(jnp.float32), axis=0)
    own_modes = lax.axis_index("mode") * local_modes + jnp.arange(local_modes, dtype=jnp.int32)
    own_onehot = ((own_modes // group_size)[:, None] == group_ids[None, :]).astype(jnp.float32)
    target_groups = jnp.arange(mode_total, dtype=jnp.int32) // group_size
    target_onehot = (target_groups[:, None] == group_ids[None, :]).astype(jnp.float32)
    own_pairs = jnp.dot(own_onehot, pair_matrix.T, precision=lax.Precision.HIGHEST)
    column_mask = jnp.dot(own_pairs, target_onehot.T, precision=lax.Precision.HIGHEST)
    shard_rows = lax.all_gather(backward, "mode", axis=0, tiled=True)
    rows_flat = shard_rows.reshape(shard_rows.shape[0], -1)
    real_part = jnp.einsum("nd,kd->nk", field_flat, rows_flat, preferred_element_type=jnp.float32)
    imag_part = jnp.einsum("nd,kd->nk", field_turned, rows_flat, preferred_element_type=jnp.float32)
    block = jnp.stack([real_part, imag_part])
    match_sum = lax.psum(block, "row")
    coupling = match_sum * (1.0 / math.sqrt(row_total * width)) * column_mask[None, :, :]
    weights = coupling.astype(jnp.bfloat16)
    shard_rows = lax.all_gather(backward, "mode", axis=0, tiled=True)
    row_count = shard_rows.shape[0]
    rows_flat = shard_rows.reshape(row_count, -1)
    rows_turned = times_i(shard_rows).reshape(row_count, -1)
    weight_real = weights[0]
    weight_imag = weights[1]
    running = jnp.dot(weight_real, rows_flat, preferred_element_type=jnp.float32)
    gathered = running + jnp.dot(weight_imag, rows_turned, preferred_element_type=jnp.float32)
    gathered = (
        (gathered * (1.0 / math.sqrt(mode_total))).astype(jnp.bfloat16).reshape(forward.shape)
    )
    padded_back = padded_2(gathered, (("row", 1),), 1)
    pulled = row_stencil(padded_back, row_taps, True).astype(jnp.bfloat16)
    adjoint = propagate(pulled, backward_matrix(propagator))
    masked_float = masked.astype(jnp.float32)
    term = masked_float[:, :, 1] * adjoint[:, :, 0] - masked_float[:, :, 0] * adjoint[:, :, 1]
    partial_grad = jnp.sum(
        term.reshape(local_modes // wave_total, wave_total, local_rows, width), axis=0
    )
    summed = lax.psum(partial_grad, "mode")
    mask_grad = summed * (-2.0 / math.sqrt(mode_total))
    return (coupling, mask_grad)


def solution(mesh):
    in_specs = (
        P("mode", "row", None, None),
        P("mode", "row", None, None),
        P(),
        P(),
        P(None, "row", None),
        P(),
        P(),
        P(),
    )
    out_specs = (P(None, "mode", None), P(None, "row", None))
    return jax.shard_map(body, mesh=mesh, in_specs=in_specs, out_specs=out_specs, check_vma=False)
```

profile of v0, /device:TPU:0, one launch (start us, length us, event | category | flops | bytes accessed | tf_op | source)
XLA Modules:
  0.0 117.6 jit_solution(7645582533571077190)
XLA Ops:
  0.6 0.0 copy-start
  0.6 0.0 copy-start.1
  0.7 0.0 copy-start.2
  0.7 0.0 copy-start.7
  0.7 0.0 copy-start.6
  0.7 2.7 %slice_bitcast_fusion = (bf16[512,512]{0,1:T(8,128)(2,1)}, bf16[512,512]{0,1:T(8,128)(2,1)}, bf16[512,512]{1,0:T(8,128)(2,1)}, bf16[512,512]{1,0:T(8,128)(2,1)}) fusion(bf16[2,512,512]{2,1,0:T(8,128)(2,1)} %param.10), kind=kLoop, calls=%fused_computation.10 | loop fusion | bytes 3145728 | tf_op jit(solution)/shard_map/transpose | solution.py:50
  3.4 0.0 copy-done.1
  3.4 0.9 fusion.19
  4.3 0.0 copy-done
  4.4 0.0 copy-done.7
  4.4 0.0 copy-done.6
  4.4 0.3 fusion.26
  4.8 1.8 %maximum_bitcast_fusion = bf16[1024,1024]{0,1:T(8,128)(2,1)S(1)} fusion(bf16[512,512]{1,0:T(8,128)(2,1)} %get-tuple-element.13, bf16[512,512]{1,0:T(8,128)(2,1)} %fusion.19, bf16[512,512]{1,0:T(8,128)(2,1)} %get-tuple-element.12), kind=kLoop, calls=%fused_computation.3 | loop fusion | flops 8388608 | bytes 3670016 | tf_op jit(solution)/shard_map/dot_general | solution.py:57
  6.6 2.6 %copy.33 = bf16[1024,1024]{1,0:T(8,128)(2,1)} copy(bf16[1024,1024]{0,1:T(8,128)(2,1)S(1)} %maximum_bitcast_fusion) | data formatting | bytes 4194304 | tf_op jit(solution)/shard_map/dot_general | solution.py:57
  9.2 2.3 %convolution_convert_fusion = bf16[8,2,2,512]{3,0,2,1:T(8,128)(2,1)S(1)} fusion(bf16[8,2,1024,1]{2,0,3,1:T(8,128)(2,1)S(1)} %bitcast.95, bf16[2,512,1024,1]{2,1,0,3:T(8,128)(2,1)} %bitcast.92), kind=kOutput, calls=%fused_computation.5 | convolution fusion | flops 33570816 | bytes 2162688 | tf_op jit(solution)/shard_map/dot_general | solution.py:57
  11.5 2.4 %collective-permute-start = (bf16[8,1,2,512]{3,0,2,1:T(8,128)(2,1)S(1)}, bf16[8,1,2,512]{3,0,2,1:T(8,128)(2,1)S(1)}, u32[]{:S(2)}, u32[]{:S(2)}) collective-permute-start(bf16[8,1,2,512]{3,0,2,1:T(8,128)(2,1)S(1)} %get-tuple-element.22), channel_id=1, source_target_pairs={{0,1},{1,2},{2,3},{4,5},{5,6},{6,7},{8,9},{9,10},{10,11},{12,13},{... | collective-permute-start | bytes 49160 | tf_op jit(solution)/shard_map/ppermute | solution.py:17
  13.9 1.3 %collective-permute-start.1 = (bf16[8,1,2,512]{3,0,2,1:T(8,128)(2,1)S(1)}, bf16[8,1,2,512]{3,0,2,1:T(8,128)(2,1)S(1)}, u32[]{:S(2)}, u32[]{:S(2)}) collective-permute-start(bf16[8,1,2,512]{3,0,2,1:T(8,128)(2,1)S(1)} %get-tuple-element.23), channel_id=1, source_target_pairs={{1,0},{2,1},{3,2},{5,4},{6,5},{7,6},{9,8},{10,9},{11,10},{13,12},{... | collective-permute-start | bytes 49160 | tf_op jit(solution)/shard_map/ppermute | solution.py:18
  15.2 0.8 fusion.20
  16.0 31.9 %all_gather.4 = bf16[64,2,2,512]{3,0,2,1:T(8,128)(2,1)S(1)} all-gather(bf16[8,2,2,512]{3,0,2,1:T(8,128)(2,1)S(1)} %copy.34), channel_id=1, replica_groups=mesh['mode'=8,'row'=4] {'mode'}, dimensions={0}, use_global_device_ids=true | all-gather | bytes 294912 | tf_op jit(solution)/shard_map/all_gather | solution.py:118
  48.0 0.1 convert_reduce_fusion
  48.1 0.2 fusion.11
  48.3 0.2 convolution_multiply_fusion.1
  48.5 0.1 pad_maximum_fusion
  48.6 1.8 %maximum_maximum_fusion = bf16[1024,1024]{0,1:T(8,128)(2,1)S(1)} fusion(bf16[512,512]{0,1:T(8,128)(2,1)} %get-tuple-element.11, bf16[512,512]{0,1:T(8,128)(2,1)} %get-tuple-element.10, bf16[512,512]{0,1:T(8,128)(2,1)} %fusion.20), kind=kLoop, calls=%fused_computation.4 | loop fusion | flops 8388608 | bytes 3670016 | tf_op jit(solution)/shard_map/concatenate | solution.py:52
  50.4 0.7 fusion.27
  51.0 0.3 copy.35
  51.3 0.2 reshape.169
  51.5 0.3 copy.36
  51.8 0.2 reshape.170
  52.0 0.0 collective-permute-done
  52.0 0.0 collective-permute-done.1
  52.0 3.7 %fusion.22 = (bf16[8,2,1,512]{3,0,2,1:T(8,128)(2,1)S(1)}, bf16[8,2,1,512]{3,0,2,1:T(8,128)(2,1)S(1)}) fusion(f32[8,4,2,512]{3,0,2,1:T(8,128)S(1)} %maximum_convert_fusion, f32[]{:T(128)} %bitcast.16, f32[]{:T(128)} %bitcast.15, f32[]{:T(128)} %bitcast.14, f32[]{:T(128)} %bitcast.13, f32[]{:T(128)} %bitcast.12, f32[]{:T(128)} %bitcast), kind=kLoop, calls=%fused_computation.70 | loop fusion | flops 106496 | bytes 229400 | tf_op jit(solution)/shard_map/neg | solution.py:91
  55.7 3.7 %add_convert_fusion.1 = bf16[8,2,1,512]{3,0,2,1:T(8,128)(2,1)S(1)} fusion(f32[8,4,2,512]{3,0,2,1:T(8,128)S(1)} %maximum_convert_fusion, f32[]{:T(128)} %bitcast.16, f32[]{:T(128)} %bitcast.15, f32[]{:T(128)} %bitcast.14, f32[]{:T(128)} %bitcast.13, f32[]{:T(128)} %bitcast.12, f32[]{:T(128)} %bitcast), kind=kLoop, calls=%fused_computation.33 | loop fusion | flops 98304 | bytes 213016 | tf_op jit(solution)/shard_map/slice | solution.py:91
  59.5 0.2 convolution_bitcast_fusion.1
  59.7 0.2 convolution_bitcast_fusion
  59.8 7.7 %psum.14 = f32[2,8,64]{2,1,0:T(8,128)S(1)} all-reduce(f32[2,8,64]{2,1,0:T(8,128)S(1)} %pad_maximum_fusion.2), channel_id=1, replica_groups=mesh['mode'=8,'row'=4] {'row'}, use_global_device_ids=true, to_apply=%region_0.0 | all-reduce | flops 1024 | bytes 8192 | tf_op jit(solution)/shard_map/psum | solution.py:123
  67.6 0.6 fusion.21
  68.2 0.1 fusion.12
  68.3 0.2 fusion.1
  68.5 2.3 %collective-permute-start.2 = (bf16[8,1,2,512]{3,0,2,1:T(8,128)(2,1)S(1)}, bf16[8,1,2,512]{3,0,2,1:T(8,128)(2,1)S(1)}, u32[]{:S(2)}, u32[]{:S(2)}) collective-permute-start(bf16[8,1,2,512]{3,0,2,1:T(8,128)(2,1)S(1)} %get-tuple-element.20), channel_id=1, source_target_pairs={{0,1},{1,2},{2,3},{4,5},{5,6},{6,7},{8,9},{9,10},{10,11},{12,13},{... | collective-permute-start | bytes 49160 | tf_op jit(solution)/shard_map/ppermute | solution.py:17
  70.8 1.3 %collective-permute-start.3 = (bf16[8,1,2,512]{3,0,2,1:T(8,128)(2,1)S(1)}, bf16[8,1,2,512]{3,0,2,1:T(8,128)(2,1)S(1)}, u32[]{:S(2)}, u32[]{:S(2)}) collective-permute-start(bf16[8,1,2,512]{3,0,2,1:T(8,128)(2,1)S(1)} %get-tuple-element.21), channel_id=1, source_target_pairs={{1,0},{2,1},{3,2},{5,4},{6,5},{7,6},{9,8},{10,9},{11,10},{13,12},{... | collective-permute-start | bytes 49160 | tf_op jit(solution)/shard_map/ppermute | solution.py:18
  72.1 0.7 fusion.28
  72.8 0.0 collective-permute-done.2
  72.8 2.6 %collective-permute-done.3 = bf16[8,1,2,512]{3,0,2,1:T(8,128)(2,1)S(1)} collective-permute-done((bf16[8,1,2,512]{3,0,2,1:T(8,128)(2,1)S(1)}, bf16[8,1,2,512]{3,0,2,1:T(8,128)(2,1)S(1)}, u32[]{:S(2)}, u32[]{:S(2)}) %collective-permute-start.3) | collective-permute-done | bytes 16416 | tf_op jit(solution)/shard_map/ppermute | solution.py:18
  75.4 3.8 %subtract_convert_fusion = (bf16[8,2,1,512]{3,0,2,1:T(8,128)(2,1)S(1)}, bf16[8,2,1,512]{3,0,2,1:T(8,128)(2,1)S(1)}) fusion(f32[8,4,2,512]{3,0,2,1:T(8,128)S(1)} %maximum_convert_fusion.1, f32[]{:T(128)} %bitcast.30, f32[]{:T(128)} %bitcast.29, f32[]{:T(128)} %bitcast.28, f32[]{:T(128)} %bitcast.15, f32[]{:T(128)} %bitcast.13, f32[]{:T(128)} %bitcast), kind=kLoop, calls=%fused_computation.31 | loop fusion | flops 196608 | bytes 229400 | tf_op jit(solution)/shard_map/convert.1
  79.2 0.6 fusion.29
  79.9 37.1 %psum.15 = f32[4,2,512]{2,0,1:T(4,128)S(1)} all-reduce(f32[4,2,512]{2,0,1:T(4,128)S(1)} %reduce_sum.19), channel_id=1, replica_groups=mesh['mode'=8,'row'=4] {'mode'}, use_global_device_ids=true, to_apply=%region_3.4 | all-reduce | flops 4096 | bytes 32768 | tf_op jit(solution)/shard_map/psum | solution.py:145
  117.0 0.6 copy.37
  (31 shorter events, 0.3 us)
Async XLA Ops:
  0.6 3.7 %copy-start = (f32[7,2,512]{2,1,0:T(2,128)S(1)}, f32[7,2,512]{2,1,0:T(2,128)}, u32[]{:S(2)}) copy-start(f32[7,2,512]{2,1,0:T(2,128)} %param.12) | copy-start | bytes 86020
  0.6 2.8 %copy-start.1 = (bf16[2,512,512]{2,1,0:T(8,128)(2,1)S(1)}, bf16[2,512,512]{2,1,0:T(8,128)(2,1)}, u32[]{:S(2)}) copy-start(bf16[2,512,512]{2,1,0:T(8,128)(2,1)} %param.10) | copy-start | bytes 3145732
  0.7 3.6 %copy-start.2 = (bf16[8,2,2,512]{3,2,1,0:T(2,128)(2,1)S(1)}, bf16[8,2,2,512]{3,2,1,0:T(2,128)(2,1)}, u32[]{:S(2)}) copy-start(bf16[8,2,2,512]{3,2,1,0:T(2,128)(2,1)} %param.8) | copy-start | bytes 98308
  0.7 3.7 %copy-start.7 = (s32[4]{0:T(128)S(1)}, s32[4]{0:T(128)}, u32[]{:S(2)}) copy-start(s32[4]{0:T(128)} %param.13) | copy-start | bytes 52
  0.7 3.7 %copy-start.6 = (f32[4]{0:T(128)S(1)}, f32[4]{0:T(128)}, u32[]{:S(2)}) copy-start(f32[4]{0:T(128)} %param.14) | copy-start | bytes 52
  9.2 6.8 %copy-start.3 = (bf16[8,2,2,512]{3,2,1,0:T(2,128)(2,1)S(1)}, bf16[8,2,2,512]{3,2,1,0:T(2,128)(2,1)}, u32[]{:S(2)}) copy-start(bf16[8,2,2,512]{3,2,1,0:T(2,128)(2,1)} %param.9) | copy-start | bytes 98308
  9.2 38.7 %copy-start.5 = (s32[80,2]{0,1:T(2,128)S(1)}, s32[80,2]{0,1:T(2,128)}, u32[]{:S(2)}) copy-start(s32[80,2]{0,1:T(2,128)} %param.15) | copy-start | bytes 1924
  9.2 38.8 %copy-start.4 = (f32[2,3]{1,0:T(2,128)S(1)}, f32[2,3]{1,0:T(2,128)}, u32[]{:S(2)}) copy-start(f32[2,3]{1,0:T(2,128)} %param.11) | copy-start | bytes 76
  11.5 40.5 %collective-permute-start = (bf16[8,1,2,512]{3,0,2,1:T(8,128)(2,1)S(1)}, bf16[8,1,2,512]{3,0,2,1:T(8,128)(2,1)S(1)}, u32[]{:S(2)}, u32[]{:S(2)}) collective-permute-start(bf16[8,1,2,512]{3,0,2,1:T(8,128)(2,1)S(1)} %get-tuple-element.22), channel_id=1, source_target_pairs={{0,1},{1,2},{2,3},{4,5},{5,6},{6,7},{8,9},{9,10},{10,11},{12,13},{... | collective-permute-start | bytes 49160 | tf_op jit(solution)/shard_map/ppermute | solution.py:17
  13.9 38.1 %collective-permute-start.1 = (bf16[8,1,2,512]{3,0,2,1:T(8,128)(2,1)S(1)}, bf16[8,1,2,512]{3,0,2,1:T(8,128)(2,1)S(1)}, u32[]{:S(2)}, u32[]{:S(2)}) collective-permute-start(bf16[8,1,2,512]{3,0,2,1:T(8,128)(2,1)S(1)} %get-tuple-element.23), channel_id=1, source_target_pairs={{1,0},{2,1},{3,2},{5,4},{6,5},{7,6},{9,8},{10,9},{11,10},{13,12},{... | collective-permute-start | bytes 49160 | tf_op jit(solution)/shard_map/ppermute | solution.py:18
  68.5 4.2 %collective-permute-start.2 = (bf16[8,1,2,512]{3,0,2,1:T(8,128)(2,1)S(1)}, bf16[8,1,2,512]{3,0,2,1:T(8,128)(2,1)S(1)}, u32[]{:S(2)}, u32[]{:S(2)}) collective-permute-start(bf16[8,1,2,512]{3,0,2,1:T(8,128)(2,1)S(1)} %get-tuple-element.20), channel_id=1, source_target_pairs={{0,1},{1,2},{2,3},{4,5},{5,6},{6,7},{8,9},{9,10},{10,11},{12,13},{... | collective-permute-start | bytes 49160 | tf_op jit(solution)/shard_map/ppermute | solution.py:17
  70.8 4.6 %collective-permute-start.3 = (bf16[8,1,2,512]{3,0,2,1:T(8,128)(2,1)S(1)}, bf16[8,1,2,512]{3,0,2,1:T(8,128)(2,1)S(1)}, u32[]{:S(2)}, u32[]{:S(2)}) collective-permute-start(bf16[8,1,2,512]{3,0,2,1:T(8,128)(2,1)S(1)} %get-tuple-element.21), channel_id=1, source_target_pairs={{1,0},{2,1},{3,2},{5,4},{6,5},{7,6},{9,8},{10,9},{11,10},{13,12},{... | collective-permute-start | bytes 49160 | tf_op jit(solution)/shard_map/ppermute | solution.py:18
where the time goes:
time: 118 us
  blocking collectives  76.7 us (65%)
  other arithmetic  17.5 us (15%)
  local copies, waits for them, and re-layouts  8.32 us (7%)
  starting transfers between devices  7.2 us (6%)
  matrix products  4.26 us (4%)
  waiting for transfers between devices  2.63 us (2%)
    psum x1, blocking collectives, body(): summed = lax.psum(partial_grad, 'mode')  37.1 us
    all_gather x1, blocking collectives, body(): shard_rows = lax.all_gather(backward, 'mode', axis=0, tiled=True)  31.9 us
    psum x1, blocking collectives, body(): match_sum = lax.psum(block, 'row')  7.74 us
    ppermute x2, starting transfers between devices, padded_2(): before = lax.ppermute(last, axis, up)  4.61 us
    another operation x2, other arithmetic  3.81 us
    neg x1, other arithmetic, times_minus_i(): return jnp.stack([fields[:, :, 1], -fields[:, :, 0]], axis=2)  3.74 us
    slice x1, other arithmetic, times_minus_i(): return jnp.stack([fields[:, :, 1], -fields[:, :, 0]], axis=2)  3.74 us
    dot_general x2, matrix products, propagate(): jnp.dot(fields.reshape(-1, 2 * width), matrix, preferred_element_type=jnp...  2.92 us
  transfers between devices with their start and end apart: 4, of which 1 were waited for; matrix products, arithmetic and copies ran while one was open for 5% of the time, Pallas kernels for 0%

commit v1 on v0

--- a/solution.py
+++ b/solution.py
@@ -142,7 +142,7 @@
     partial_grad = jnp.sum(
         term.reshape(local_modes // wave_total, wave_total, local_rows, width), axis=0
     )
-    summed = lax.psum(partial_grad, "mode")
+    summed = jnp.sum(lax.all_gather(partial_grad, "mode"), axis=0)
     mask_grad = summed * (-2.0 / math.sqrt(mode_total))
     return (coupling, mask_grad)
 

time: 118 us -> 114 us (0.966)
  blocking collectives: 76.7 us -> 70.2 us
    psum x1 -> x0, blocking collectives: 37.1 us -> none  [body(): summed = lax.psum(partial_grad, 'mode')]
    all_gather x0 -> x1, blocking collectives: none -> 30.5 us  [body(): summed = jnp.sum(lax.all_gather(partial_grad, 'mode'), axis=0)]
  transfers between devices with their start and end apart: 4 -> 4, of which waited for: 1 -> 1; matrix products, arithmetic and copies ran while one was open for 5% -> 6% of each run, Pallas kernels for 0% -> 0%
where the time goes in v1:
time: 114 us; the launch traced here: 113 us
  blocking collectives  70.2 us (62%)
  other arithmetic  18.1 us (16%)
  local copies, waits for them, and re-layouts  9.32 us (8%)
  starting transfers between devices  7.19 us (6%)
  matrix products  4.93 us (4%)
  waiting for transfers between devices  2.62 us (2%)
    all_gather x1, blocking collectives, body(): shard_rows = lax.all_gather(backward, 'mode', axis=0, tiled=True)  31.9 us
    all_gather x1, blocking collectives, body(): summed = jnp.sum(lax.all_gather(partial_grad, 'mode'), axis=0)  30.5 us
    psum x1, blocking collectives, body(): match_sum = lax.psum(block, 'row')  7.74 us
    ppermute x2, starting transfers between devices, padded_2(): before = lax.ppermute(last, axis, up)  4.6 us
    another operation x2, other arithmetic  3.76 us
    neg x1, other arithmetic, times_minus_i(): return jnp.stack([fields[:, :, 1], -fields[:, :, 0]], axis=2)  3.72 us
    slice x1, other arithmetic, times_minus_i(): return jnp.stack([fields[:, :, 1], -fields[:, :, 0]], axis=2)  3.71 us
    dot_general x2, matrix products, propagate(): jnp.dot(fields.reshape(-1, 2 * width), matrix, preferred_element_type=jnp...  2.94 us
  transfers between devices with their start and end apart: 4, of which 1 were waited for; matrix products, arithmetic and copies ran while one was open for 6% of the time, Pallas kernels for 0%

profile of v1, /device:TPU:0, one launch (start us, length us, event | category | flops | bytes accessed | tf_op | source)
XLA Modules:
  0.0 113.4 jit_solution(6418136034371616115)
XLA Ops:
  0.6 0.0 copy-start
  0.6 0.0 copy-start.1
  0.7 0.0 copy-start.3
  0.7 0.0 copy-start.10
  0.7 0.0 copy-start.9
  0.7 2.7 %slice_bitcast_fusion = (bf16[512,512]{0,1:T(8,128)(2,1)}, bf16[512,512]{0,1:T(8,128)(2,1)}, bf16[512,512]{1,0:T(8,128)(2,1)}, bf16[512,512]{1,0:T(8,128)(2,1)}) fusion(bf16[2,512,512]{2,1,0:T(8,128)(2,1)} %param.10), kind=kLoop, calls=%fused_computation.10 | loop fusion | bytes 3145728 | tf_op jit(solution)/shard_map/transpose | solution.py:50
  3.4 0.0 copy-done.1
  3.4 0.9 fusion.19
  4.3 0.0 copy-done.3
  4.4 0.3 fusion.26
  4.8 1.8 %maximum_bitcast_fusion = bf16[1024,1024]{0,1:T(8,128)(2,1)S(1)} fusion(bf16[512,512]{1,0:T(8,128)(2,1)} %get-tuple-element.9, bf16[512,512]{1,0:T(8,128)(2,1)} %fusion.19, bf16[512,512]{1,0:T(8,128)(2,1)} %get-tuple-element.8), kind=kLoop, calls=%fused_computation.3 | loop fusion | flops 8388608 | bytes 3670016 | tf_op jit(solution)/shard_map/dot_general | solution.py:57
  6.6 2.6 %copy.33 = bf16[1024,1024]{1,0:T(8,128)(2,1)} copy(bf16[1024,1024]{0,1:T(8,128)(2,1)S(1)} %maximum_bitcast_fusion) | data formatting | bytes 4194304 | tf_op jit(solution)/shard_map/dot_general | solution.py:57
  9.2 2.3 %convolution_convert_fusion = bf16[8,2,2,512]{3,0,2,1:T(8,128)(2,1)S(1)} fusion(bf16[8,2,1024,1]{2,0,3,1:T(8,128)(2,1)S(1)} %bitcast.97, bf16[2,512,1024,1]{2,1,0,3:T(8,128)(2,1)} %bitcast.93), kind=kOutput, calls=%fused_computation.5 | convolution fusion | flops 33570816 | bytes 2162688 | tf_op jit(solution)/shard_map/dot_general | solution.py:57
  11.5 0.6 fusion.24
  12.1 2.3 %collective-permute-start = (bf16[8,1,2,512]{3,0,2,1:T(8,128)(2,1)}, bf16[8,1,2,512]{3,0,2,1:T(8,128)(2,1)S(1)}, u32[]{:S(2)}, u32[]{:S(2)}) collective-permute-start(bf16[8,1,2,512]{3,0,2,1:T(8,128)(2,1)} %get-tuple-element.18), channel_id=1, source_target_pairs={{0,1},{1,2},{2,3},{4,5},{5,6},{6,7},{8,9},{9,10},{10,11},{12,13},{... | collective-permute-start | bytes 49160 | tf_op jit(solution)/shard_map/ppermute | solution.py:17
  14.5 1.3 %collective-permute-start.1 = (bf16[8,1,2,512]{3,0,2,1:T(8,128)(2,1)S(1)}, bf16[8,1,2,512]{3,0,2,1:T(8,128)(2,1)S(1)}, u32[]{:S(2)}, u32[]{:S(2)}) collective-permute-start(bf16[8,1,2,512]{3,0,2,1:T(8,128)(2,1)S(1)} %get-tuple-element.19), channel_id=1, source_target_pairs={{1,0},{2,1},{3,2},{5,4},{6,5},{7,6},{9,8},{10,9},{11,10},{13,12},{... | collective-permute-start | bytes 49160 | tf_op jit(solution)/shard_map/ppermute | solution.py:18
  15.9 31.9 %all_gather.10 = bf16[64,2,2,512]{3,0,2,1:T(8,128)(2,1)S(1)} all-gather(bf16[8,2,2,512]{3,0,2,1:T(8,128)(2,1)S(1)} %copy.34), channel_id=1, replica_groups=mesh['mode'=8,'row'=4] {'mode'}, dimensions={0}, use_global_device_ids=true | all-gather | bytes 294912 | tf_op jit(solution)/shard_map/all_gather | solution.py:118
  47.8 0.6 slice_negate_fusion.1
  48.4 0.1 convert_reduce_fusion
  48.5 0.2 fusion.11
  48.7 0.8 convolution_multiply_fusion.1
  49.5 0.7 pad_maximum_fusion
  50.3 1.5 %maximum_maximum_fusion = bf16[1024,1024]{0,1:T(8,128)(2,1)S(1)} fusion(bf16[512,512]{0,1:T(8,128)(2,1)} %get-tuple-element.7, bf16[512,512]{0,1:T(8,128)(2,1)S(1)} %copy-done.2, bf16[512,512]{0,1:T(8,128)(2,1)S(1)} %fusion.20), kind=kLoop, calls=%fused_computation.4 | loop fusion | flops 8388608 | bytes 3670016 | tf_op jit(solution)/shard_map/concatenate | solution.py:52
  51.7 0.0 copy-start.7
  51.8 0.7 fusion.27
  52.4 0.3 copy.35
  52.7 0.2 reshape.169
  52.9 1.2 %copy.36 = bf16[64,2,2,512]{3,2,1,0:T(2,128)(2,1)S(1)} copy(bf16[64,2,2,512]{3,0,2,1:T(8,128)(2,1)} %pad_maximum_fusion) | data formatting | bytes 524288 | tf_op jit(solution)/shard_map/stack | solution.py:87
  54.1 0.2 reshape.170
  54.3 0.0 collective-permute-done
  54.3 0.0 collective-permute-done.1
  54.3 3.7 %fusion.22 = (bf16[8,2,1,512]{3,0,2,1:T(8,128)(2,1)S(1)}, bf16[8,2,1,512]{3,0,2,1:T(8,128)(2,1)S(1)}) fusion(f32[8,4,2,512]{3,0,2,1:T(8,128)S(1)} %maximum_convert_fusion, f32[]{:T(128)} %bitcast.16, f32[]{:T(128)} %bitcast.15, f32[]{:T(128)} %bitcast.14, f32[]{:T(128)} %bitcast.13, f32[]{:T(128)} %bitcast.12, f32[]{:T(128)} %bitcast), kind=kLoop, calls=%fused_computation.70 | loop fusion | flops 106496 | bytes 229400 | tf_op jit(solution)/shard_map/neg | solution.py:91
  58.1 3.7 %add_convert_fusion.1 = bf16[8,2,1,512]{3,0,2,1:T(8,128)(2,1)S(1)} fusion(f32[8,4,2,512]{3,0,2,1:T(8,128)S(1)} %maximum_convert_fusion, f32[]{:T(128)} %bitcast.16, f32[]{:T(128)} %bitcast.15, f32[]{:T(128)} %bitcast.14, f32[]{:T(128)} %bitcast.13, f32[]{:T(128)} %bitcast.12, f32[]{:T(128)} %bitcast), kind=kLoop, calls=%fused_computation.33 | loop fusion | flops 98304 | bytes 213016 | tf_op jit(solution)/shard_map/slice | solution.py:91
  61.8 0.2 convolution_bitcast_fusion.1
  61.9 0.2 convolution_bitcast_fusion
  62.1 7.7 %psum.7 = f32[2,8,64]{2,1,0:T(8,128)S(1)} all-reduce(f32[2,8,64]{2,1,0:T(8,128)S(1)} %pad_maximum_fusion.2), channel_id=1, replica_groups=mesh['mode'=8,'row'=4] {'row'}, use_global_device_ids=true, to_apply=%region_0.0 | all-reduce | flops 1024 | bytes 8192 | tf_op jit(solution)/shard_map/psum | solution.py:123
  69.9 0.6 fusion.21
  70.5 0.1 fusion.12
  70.6 0.2 fusion.1
  70.8 2.3 %collective-permute-start.2 = (bf16[8,1,2,512]{3,0,2,1:T(8,128)(2,1)S(1)}, bf16[8,1,2,512]{3,0,2,1:T(8,128)(2,1)S(1)}, u32[]{:S(2)}, u32[]{:S(2)}) collective-permute-start(bf16[8,1,2,512]{3,0,2,1:T(8,128)(2,1)S(1)} %get-tuple-element.16), channel_id=1, source_target_pairs={{0,1},{1,2},{2,3},{4,5},{5,6},{6,7},{8,9},{9,10},{10,11},{12,13},{... | collective-permute-start | bytes 49160 | tf_op jit(solution)/shard_map/ppermute | solution.py:17
  73.1 1.3 %collective-permute-start.3 = (bf16[8,1,2,512]{3,0,2,1:T(8,128)(2,1)S(1)}, bf16[8,1,2,512]{3,0,2,1:T(8,128)(2,1)S(1)}, u32[]{:S(2)}, u32[]{:S(2)}) collective-permute-start(bf16[8,1,2,512]{3,0,2,1:T(8,128)(2,1)S(1)} %get-tuple-element.17), channel_id=1, source_target_pairs={{1,0},{2,1},{3,2},{5,4},{6,5},{7,6},{9,8},{10,9},{11,10},{13,12},{... | collective-permute-start | bytes 49160 | tf_op jit(solution)/shard_map/ppermute | solution.py:18
  74.4 0.7 fusion.28
  75.1 0.0 collective-permute-done.2
  75.1 2.6 %collective-permute-done.3 = bf16[8,1,2,512]{3,0,2,1:T(8,128)(2,1)S(1)} collective-permute-done((bf16[8,1,2,512]{3,0,2,1:T(8,128)(2,1)S(1)}, bf16[8,1,2,512]{3,0,2,1:T(8,128)(2,1)S(1)}, u32[]{:S(2)}, u32[]{:S(2)}) %collective-permute-start.3) | collective-permute-done | bytes 16416 | tf_op jit(solution)/shard_map/ppermute | solution.py:18
  77.7 3.7 %subtract_convert_fusion = (bf16[8,2,1,512]{3,0,2,1:T(8,128)(2,1)S(1)}, bf16[8,2,1,512]{3,0,2,1:T(8,128)(2,1)S(1)}) fusion(f32[8,4,2,512]{3,0,2,1:T(8,128)S(1)} %maximum_convert_fusion.1, f32[]{:T(128)} %bitcast.30, f32[]{:T(128)} %bitcast.29, f32[]{:T(128)} %bitcast.28, f32[]{:T(128)} %bitcast.15, f32[]{:T(128)} %bitcast.13, f32[]{:T(128)} %bitcast), kind=kLoop, calls=%fused_computation.31 | loop fusion | flops 196608 | bytes 229400 | tf_op jit(solution)/shard_map/convert.1
  81.5 0.6 fusion.29
  82.2 30.5 %all-gather = f32[32,2,512]{2,1,0:T(2,128)S(1)} all-gather(f32[4,2,512]{2,1,0:T(2,128)S(1)} %copy.37), channel_id=2, replica_groups=mesh['mode'=8,'row'=4] {'mode'}, dimensions={0}, use_global_device_ids=true | all-gather | bytes 147456 | tf_op jit(solution)/shard_map/all_gather | solution.py:145
  112.8 0.6 broadcast_multiply_fusion
  (38 shorter events, 0.4 us)
Async XLA Ops:
  0.6 3.7 %copy-start = (f32[7,2,512]{2,1,0:T(2,128)S(1)}, f32[7,2,512]{2,1,0:T(2,128)}, u32[]{:S(2)}) copy-start(f32[7,2,512]{2,1,0:T(2,128)} %param.12) | copy-start | bytes 86020
  0.6 2.8 %copy-start.1 = (bf16[2,512,512]{2,1,0:T(8,128)(2,1)S(1)}, bf16[2,512,512]{2,1,0:T(8,128)(2,1)}, u32[]{:S(2)}) copy-start(bf16[2,512,512]{2,1,0:T(8,128)(2,1)} %param.10) | copy-start | bytes 3145732
  0.7 3.6 %copy-start.3 = (bf16[8,2,2,512]{3,2,1,0:T(2,128)(2,1)S(1)}, bf16[8,2,2,512]{3,2,1,0:T(2,128)(2,1)}, u32[]{:S(2)}) copy-start(bf16[8,2,2,512]{3,2,1,0:T(2,128)(2,1)} %param.8) | copy-start | bytes 98308
  0.7 3.7 %copy-start.10 = (s32[4]{0:T(128)S(1)}, s32[4]{0:T(128)}, u32[]{:S(2)}) copy-start(s32[4]{0:T(128)} %param.13) | copy-start | bytes 52
  0.7 3.7 %copy-start.9 = (f32[4]{0:T(128)S(1)}, f32[4]{0:T(128)}, u32[]{:S(2)}) copy-start(f32[4]{0:T(128)} %param.14) | copy-start | bytes 52
  9.2 6.7 %copy-start.4 = (bf16[8,2,2,512]{3,2,1,0:T(2,128)(2,1)S(1)}, bf16[8,2,2,512]{3,2,1,0:T(2,128)(2,1)}, u32[]{:S(2)}) copy-start(bf16[8,2,2,512]{3,2,1,0:T(2,128)(2,1)} %param.9) | copy-start | bytes 98308
  9.2 38.6 %copy-start.8 = (s32[80,2]{0,1:T(2,128)S(1)}, s32[80,2]{0,1:T(2,128)}, u32[]{:S(2)}) copy-start(s32[80,2]{0,1:T(2,128)} %param.15) | copy-start | bytes 1924
  9.2 38.6 %copy-start.5 = (f32[2,3]{1,0:T(2,128)S(1)}, f32[2,3]{1,0:T(2,128)}, u32[]{:S(2)}) copy-start(f32[2,3]{1,0:T(2,128)} %param.11) | copy-start | bytes 76
  9.2 41.1 %copy-start.2 = (bf16[512,512]{0,1:T(8,128)(2,1)S(1)}, bf16[512,512]{0,1:T(8,128)(2,1)}, u32[]{:S(2)}) copy-start(bf16[512,512]{0,1:T(8,128)(2,1)} %get-tuple-element.6) | copy-start | bytes 1572868
  12.1 42.2 %collective-permute-start = (bf16[8,1,2,512]{3,0,2,1:T(8,128)(2,1)}, bf16[8,1,2,512]{3,0,2,1:T(8,128)(2,1)S(1)}, u32[]{:S(2)}, u32[]{:S(2)}) collective-permute-start(bf16[8,1,2,512]{3,0,2,1:T(8,128)(2,1)} %get-tuple-element.18), channel_id=1, source_target_pairs={{0,1},{1,2},{2,3},{4,5},{5,6},{6,7},{8,9},{9,10},{10,11},{12,13},{... | collective-permute-start | bytes 49160 | tf_op jit(solution)/shard_map/ppermute | solution.py:17
  14.5 39.8 %collective-permute-start.1 = (bf16[8,1,2,512]{3,0,2,1:T(8,128)(2,1)S(1)}, bf16[8,1,2,512]{3,0,2,1:T(8,128)(2,1)S(1)}, u32[]{:S(2)}, u32[]{:S(2)}) collective-permute-start(bf16[8,1,2,512]{3,0,2,1:T(8,128)(2,1)S(1)} %get-tuple-element.19), channel_id=1, source_target_pairs={{1,0},{2,1},{3,2},{5,4},{6,5},{7,6},{9,8},{10,9},{11,10},{13,12},{... | collective-permute-start | bytes 49160 | tf_op jit(solution)/shard_map/ppermute | solution.py:18
  51.7 18.1 %copy-start.7 = (f32[8,64]{1,0:T(8,128)S(1)}, f32[8,64]{1,0:T(8,128)}, u32[]{:S(2)}) copy-start(f32[8,64]{1,0:T(8,128)} %convolution_multiply_fusion.1) | copy-start | bytes 6148
  51.7 22.6 %copy-start.6 = (f32[1,3]{1,0:T(1,128)S(1)}, f32[1,3]{1,0:T(1,128)}, u32[]{:S(2)}) copy-start(f32[1,3]{1,0:T(1,128)} %slice_negate_fusion.1) | copy-start | bytes 40
  70.8 4.2 %collective-permute-start.2 = (bf16[8,1,2,512]{3,0,2,1:T(8,128)(2,1)S(1)}, bf16[8,1,2,512]{3,0,2,1:T(8,128)(2,1)S(1)}, u32[]{:S(2)}, u32[]{:S(2)}) collective-permute-start(bf16[8,1,2,512]{3,0,2,1:T(8,128)(2,1)S(1)} %get-tuple-element.16), channel_id=1, source_target_pairs={{0,1},{1,2},{2,3},{4,5},{5,6},{6,7},{8,9},{9,10},{10,11},{12,13},{... | collective-permute-start | bytes 49160 | tf_op jit(solution)/shard_map/ppermute | solution.py:17
  73.1 4.6 %collective-permute-start.3 = (bf16[8,1,2,512]{3,0,2,1:T(8,128)(2,1)S(1)}, bf16[8,1,2,512]{3,0,2,1:T(8,128)(2,1)S(1)}, u32[]{:S(2)}, u32[]{:S(2)}) collective-permute-start(bf16[8,1,2,512]{3,0,2,1:T(8,128)(2,1)S(1)} %get-tuple-element.17), channel_id=1, source_target_pairs={{1,0},{2,1},{3,2},{5,4},{6,5},{7,6},{9,8},{10,9},{11,10},{13,12},{... | collective-permute-start | bytes 49160 | tf_op jit(solution)/shard_map/ppermute | solution.py:18
